TPU v7x, 128 devices: a whole 4x4x4 slice. The times are simulated.
128 devices in a mesh: seq: 16 (over x_hi, y, core), fsdp: 2 (over x_lo), dp: 4 (over z).
Axes of the slice: x: 4 (x_hi: 2, x_lo: 2; x = x_hi * 2 + x_lo), y: 4, z: 4, core: 2. Of those that a mesh axis runs over, the one named last changes fastest.
Arguments:
- queries: bfloat16 [8, 4096, 4096], P(('fsdp', 'dp'), 'seq'), may hold values from -160 to 160
- hidden: bfloat16 [8, 4096, 8192], P(('fsdp', 'dp'), 'seq'), may hold values from -8 to 8
- key_weight: bfloat16 [8192, 512], P('fsdp'), may hold values from -1 to 1
- doc_lengths: int32 [8, 32], P(('fsdp', 'dp')), may hold values from 1 to 256, 4096 in all within a row
- entropy_cot: bfloat16 [8, 4096, 32], P(('fsdp', 'dp'), 'seq'), may hold values from -600 to 600
Outputs:
- entropy: float32 [8, 4096, 32], P(('fsdp', 'dp'), 'seq')
- grad_queries: bfloat16 [8, 4096, 4096], P(('fsdp', 'dp'), 'seq')
- grad_key_weight: bfloat16 [8192, 512], P('fsdp')
Inputs may be any that keep to these rules, and one draw needn't show every extreme that they name: `doc_lengths`: each sequence's 32 documents are packed in order, their lengths sum to 4096, and the longest is exactly 256.
All inputs are finite; a program needn't handle non-finite values.
Results may differ from a plain program's by a relative error of at most 0.0088.
Values may be sent and summed in bfloat16 or wider, within the bound.
No kernel may reach another device: no remote copies, remote signals or barrier semaphores. Data moves between devices by JAX's collectives and lax.ppermute only.
A program may use at most 128 MiB of HBM per device.

v0:
```python
import jax
import jax.numpy as jnp
from jax import lax
from jax.sharding import PartitionSpec as P

QH = 32
KVH = 4
HD = 128


def document_index(lengths, seq_len):
    ends = jnp.cumsum(lengths)
    position = jnp.arange(seq_len, dtype=jnp.int32)
    return jnp.sum((ends[None, :] <= position[:, None]).astype(jnp.int32), axis=1)


def attend(queries, key_rows, cotangent, doc_index, doc_len):
    row_count, key_heads, group_size, head_size = queries.shape
    full_len = key_rows.shape[0]
    block_rows = min(512, row_count)
    window = block_rows + doc_len
    factor = head_size ** (-0.5)
    keys_padded = jnp.concatenate(
        [jnp.zeros((doc_len, key_heads, head_size), key_rows.dtype), key_rows], axis=0
    )
    index_padded = jnp.concatenate([jnp.full((doc_len,), -1, jnp.int32), doc_index], axis=0)

    def one_block(step_index, state_now):
        entropy, grad_query, grad_key = state_now
        row_start = (step_index * block_rows).astype(jnp.int32)
        query_block = lax.dynamic_slice_in_dim(queries, row_start, block_rows, 0)
        weight_block = lax.dynamic_slice_in_dim(cotangent, row_start, block_rows, 0).astype(
            jnp.float32
        )
        key_block = lax.dynamic_slice_in_dim(keys_padded, row_start, window, 0)
        key_docs = lax.dynamic_slice_in_dim(index_padded, row_start, window, 0)
        query_docs = lax.dynamic_slice_in_dim(doc_index, row_start, block_rows, 0)
        query_pos = row_start + jnp.arange(block_rows, dtype=jnp.int32)
        key_pos = row_start - doc_len + jnp.arange(window, dtype=jnp.int32)
        visible = (query_docs[:, None] == key_docs[None, :]) & (
            key_pos[None, :] <= query_pos[:, None]
        )
        scores = (
            jnp.einsum("rkgd,wkd->kgrw", query_block, key_block, preferred_element_type=jnp.float32)
            * factor
        )
        scores = jnp.where(visible, scores, -1e30)
        row_max = jnp.max(scores, axis=-1, keepdims=True)
        powers = jnp.exp(scores - row_max)
        denominator = jnp.sum(powers, axis=-1, keepdims=True)
        probability = powers / denominator
        mean_score = jnp.sum(jnp.where(visible, probability * scores, 0.0), axis=-1, keepdims=True)
        block_entropy = (row_max + jnp.log(denominator) - mean_score)[..., 0]
        row_weight = jnp.transpose(weight_block, (1, 2, 0))[..., None]
        slope = jnp.where(visible, row_weight * probability * (mean_score - scores), 0.0).astype(
            jnp.bfloat16
        )
        query_part = (
            jnp.einsum("kgrw,wkd->rkgd", slope, key_block, preferred_element_type=jnp.float32)
            * factor
        )
        key_part = (
            jnp.einsum("kgrw,rkgd->wkd", slope, query_block, preferred_element_type=jnp.float32)
            * factor
        )
        entropy = lax.dynamic_update_slice_in_dim(
            entropy, jnp.transpose(block_entropy, (2, 0, 1)), row_start, 0
        )
        grad_query = lax.dynamic_update_slice_in_dim(grad_query, query_part, row_start, 0)
        previous = lax.dynamic_slice_in_dim(grad_key, row_start, window, 0)
        grad_key = lax.dynamic_update_slice_in_dim(grad_key, previous + key_part, row_start, 0)
        return (entropy, grad_query, grad_key)

    initial = (
        jnp.zeros((row_count, key_heads, group_size), jnp.float32),
        jnp.zeros((row_count, key_heads, group_size, head_size), jnp.float32),
        jnp.zeros((full_len + doc_len, key_heads, head_size), jnp.float32),
    )
    entropy, grad_query, grad_key = lax.fori_loop(0, row_count // block_rows, one_block, initial)
    return (entropy, grad_query, grad_key[doc_len:])


def shards(queries, hidden, key_weight, doc_lengths, entropy_cot):
    tokens = hidden[0]
    local_rows = tokens.shape[0]
    seq_parts = lax.axis_size("seq")
    seq_len = local_rows * seq_parts
    group_size = QH // KVH
    doc_index = document_index(doc_lengths[0], seq_len)
    columns = tokens
    key_local = jnp.dot(
        columns,
        lax.all_gather(key_weight, "fsdp", axis=0, tiled=True),
        preferred_element_type=jnp.float32,
    ).astype(jnp.bfloat16)
    query_local = queries[0]
    cot_local = entropy_cot[0]
    share = QH // seq_parts
    outgoing = jnp.broadcast_to(
        key_local.reshape(local_rows, KVH, 1, HD), (local_rows, KVH, group_size, HD)
    )
    outgoing = outgoing.reshape(local_rows, KVH * group_size * HD)
    query_heads, key_heads_seq, cot_heads = (
        lax.all_to_all(query_local, "seq", split_axis=1, concat_axis=0, tiled=True),
        lax.all_to_all(outgoing, "seq", split_axis=1, concat_axis=0, tiled=True),
        lax.all_to_all(cot_local, "seq", split_axis=1, concat_axis=0, tiled=True),
    )
    key_count = key_heads_seq.shape[1] // HD
    entropy, grad_query, grad_key = attend(
        query_heads.reshape(seq_len, key_count, share // key_count, HD),
        key_heads_seq.reshape(seq_len, key_count, HD),
        cot_heads.reshape(seq_len, key_count, share // key_count),
        doc_index,
        local_rows,
    )
    grad_local, key_grad_local, entropy_local = (
        lax.all_to_all(
            grad_query.reshape(seq_len, share * HD), "seq", split_axis=0, concat_axis=1, tiled=True
        ),
        lax.all_to_all(
            grad_key.reshape(seq_len, key_count * HD),
            "seq",
            split_axis=0,
            concat_axis=1,
            tiled=True,
        ),
        lax.all_to_all(
            entropy.reshape(seq_len, share), "seq", split_axis=0, concat_axis=1, tiled=True
        ),
    )
    key_grad = jnp.sum(key_grad_local.reshape(local_rows, KVH, -1, HD), axis=2).reshape(
        local_rows, KVH * HD
    )
    key_grad_low = key_grad.astype(jnp.bfloat16)
    columns = tokens
    term_rows = lax.psum_scatter(
        lax.dot_general(
            columns, key_grad_low, (((0,), (0,)), ((), ())), preferred_element_type=jnp.float32
        ),
        "fsdp",
        scatter_dimension=0,
        tiled=True,
    )
    summed = lax.psum(term_rows, ("seq", "dp"))
    norm_factor = (seq_len * lax.axis_size("fsdp") * lax.axis_size("dp")) ** (-0.5)
    weight_grad = (summed * norm_factor).astype(jnp.bfloat16)
    return (
        entropy_local.reshape(1, local_rows, QH),
        grad_local.astype(jnp.bfloat16).reshape(1, local_rows, QH * HD),
        weight_grad,
    )


def solution(mesh):
    return jax.shard_map(
        shards,
        mesh=mesh,
        in_specs=(
            P(("fsdp", "dp"), "seq", None),
            P(("fsdp", "dp"), "seq", None),
            P("fsdp", None),
            P(("fsdp", "dp"), None),
            P(("fsdp", "dp"), "seq", None),
        ),
        out_specs=(P(("fsdp", "dp"), "seq", None), P(("fsdp", "dp"), "seq", None), P("fsdp", None)),
        check_vma=False,
    )
```

profile of v0, /device:TPU:0, one launch (start us, length us, event | category | flops | bytes accessed | tf_op | source)
XLA Modules:
  0.0 1256.6 jit_solution(18081824443787886025)
XLA Ops:
  8.8 2.4 copy.83
  11.2 7.1 all-to-all-start.1
  18.3 114.7 %all-gather.2.cloned.1.call-done = bf16[8192,512]{1,0:T(8,128)(2,1)} async-done(((bf16[4096,512]{1,0:T(8,128)(2,1)}), bf16[8192,512]{1,0:T(8,128)(2,1)}) %all-gather.2.cloned.1.call-update) | async-done | bytes 8388624 | tf_op jit(solution)/shard_map/all_gather | solution.py:93
  133.0 7.0 fusion.41
  140.1 1.6 broadcast_in_dim.83
  141.7 8.3 all-to-all-start
  150.9 28.5 %all-to-all-done = bf16[256,16,256]{0,2,1:T(8,128)(2,1)} async-done(((bf16[256,16,256]{0,2,1:T(8,128)(2,1)}), bf16[256,16,256]{0,2,1:T(8,128)(2,1)}, u32[]{:S(2)}, u32[]{:S(2)}) %all-to-all-start) | async-done | bytes 2097184 | tf_op jit(solution)/shard_map/all_to_all | solution.py:105
  179.3 6.3 all-to-all-start.2
  186.0 2.5 copy.84
  188.5 4.2 reshape.222
  192.7 4.1 copy.82
  196.8 2.9 reshape.221
  199.7 1.5 concatenate.7
  202.1 2.3 broadcast_in_dim.81
  204.4 88.0 %while.19 = (s32[]{:T(128)}, f32[4096,2,1]{0,1,2:T(2,128)}, bf16[4096,2,1,128]{0,3,1,2:T(8,128)(2,1)S(1)}, f32[4352,2,128]{0,2,1:T(8,128)}, s32[4096]{0:T(1024)S...) while((s32[]{:T(128)}, f32[4096,2,1]{0,1,2:T(2,128)}, ...), condition=%wide.region_6.7_spmd, body=%wide.region_2.6_spmd.sunk | while | flops 630850816 | bytes 21601552 | solution.py:79
  205.0 1.9 fusion.58
  207.6 1.0 select_reduce_fusion.2
  209.3 2.5 fusion.60
  211.7 3.7 fusion.61
  216.0 1.9 fusion.58
  218.6 1.0 select_reduce_fusion.2
  220.3 2.5 fusion.60
  222.7 3.6 fusion.61
  226.9 1.9 fusion.58
  229.6 1.0 select_reduce_fusion.2
  231.2 2.5 fusion.60
  233.7 3.7 fusion.61
  237.9 1.9 fusion.58
  240.6 1.0 select_reduce_fusion.2
  242.3 2.5 fusion.60
  244.7 3.7 fusion.61
  248.9 1.9 fusion.58
  253.3 2.5 fusion.60
  255.7 3.7 fusion.61
  259.9 1.9 fusion.58
  262.6 1.0 select_reduce_fusion.2
  264.3 2.5 fusion.60
  266.7 3.7 fusion.61
  270.9 1.9 fusion.58
  273.6 1.0 select_reduce_fusion.2
  275.3 2.5 fusion.60
  277.7 3.7 fusion.61
  281.9 1.9 fusion.58
  284.6 1.0 select_reduce_fusion.2
  286.3 2.5 fusion.60
  288.7 3.7 fusion.61
  292.4 2.5 slice.3
  294.9 1.7 copy.102
  296.6 2.4 copy.90
  299.1 58.8 %all_to_all.93 = f32[16,256,256]{1,2,0:T(8,128)} all-to-all(f32[16,256,256]{1,2,0:T(8,128)S(1)} %copy.90), channel_id=1, replica_groups=mesh['seq'=16,'fsdp'=2,'dp'=4] {'seq'}, dimensions={0} | all-to-all | bytes 8388608 | tf_op jit(solution)/shard_map/all_to_all | solution.py:120
  357.9 2.5 reduce_sum.41
  360.4 10.3 convolution_bitcast_fusion
  370.7 189.8 %reduce-scatter.2.cloned.1.call-done = f32[4096,512]{0,1:T(8,128)} async-done(((f32[8192,512]{0,1:T(8,128)}), f32[4096,512]{0,1:T(8,128)}) %reduce-scatter.2.cloned.1.call-update) | async-done | bytes 8388624 | tf_op jit(solution)/shard_map/reduce_scatter | solution.py:136
  560.6 6.5 all-to-all-start.3
  567.1 2.0 copy.101
  569.1 4.3 copy.98
  573.3 1.4 all-to-all-done.3
  574.7 5.9 all-to-all-start.4
  581.2 29.5 %all-to-all-done.4 = bf16[16,256,256]{2,1,0:T(8,128)(2,1)S(1)} async-done(((bf16[16,256,256]{2,1,0:T(8,128)(2,1)}), bf16[16,256,256]{2,1,0:T(8,128)(2,1)S(1)}, u32[]{:S(2)}, u32[]{:S(2)}) %all-to-all-start.4) | async-done | bytes 2097184 | tf_op jit(solution)/shard_map/all_to_all | solution.py:117
  610.7 2.4 copy.89
  613.0 4.1 copy.91
  617.1 620.1 %all-reduce.4.cloned.1.call-done = f32[4096,512]{0,1:T(8,128)} async-done(((f32[4096,512]{0,1:T(8,128)}), f32[4096,512]{0,1:T(8,128)}) %all-reduce.4.cloned.1.call-update) | async-done | bytes 8388624 | tf_op jit(solution)/shard_map/psum | solution.py:144
  1237.3 6.4 multiply_convert_fusion
  1243.6 6.4 copy.92
  (89 shorter events, 20.7 us)
Async XLA Ops:
  7.2 1.6 copy-start
  7.2 125.8 %all-gather.2.cloned.1.call-start = ((), (), s32[]{:S(2)}) async-start(), calls=%async_computation.7 | async-start | bytes 12582912 | tf_op jit(solution)/shard_map/all_gather | solution.py:93
  11.2 128.9 %all-to-all-start.1 = ((bf16[256,16,256]{0,2,1:T(8,128)(2,1)}), bf16[256,16,256]{0,2,1:T(8,128)(2,1)S(1)}, u32[]{:S(2)}, u32[]{:S(2)}) async-start(bf16[256,16,256]{0,2,1:T(8,128)(2,1)} %bitcast.144), calls=%async_computation.1 | async-start | bytes 4194304 | tf_op jit(solution)/shard_map/all_to_all | solution.py:104
  140.1 9.9 copy-start.2
  140.1 10.1 copy-start.1
  141.7 37.6 %all-to-all-start = ((bf16[256,16,256]{0,2,1:T(8,128)(2,1)}), bf16[256,16,256]{0,2,1:T(8,128)(2,1)}, u32[]{:S(2)}, u32[]{:S(2)}) async-start(bf16[256,16,256]{0,2,1:T(8,128)(2,1)} %bitcast.145), calls=%async_computation | async-start | bytes 4194304 | tf_op jit(solution)/shard_map/all_to_all | solution.py:105
  179.3 21.9 %all-to-all-start.2 = ((bf16[256,16,2]{0,2,1:T(2,128)(2,1)}), bf16[256,16,2]{0,2,1:T(2,128)(2,1)S(1)}, u32[]{:S(2)}, u32[]{:S(2)}) async-start(bf16[256,16,2]{0,2,1:T(2,128)(2,1)} %all_to_all.76), calls=%async_computation.2 | async-start | bytes 32768 | tf_op jit(solution)/shard_map/all_to_all | solution.py:106
  185.6 374.9 %reduce-scatter.2.cloned.1.call-start = ((), (), s32[]{:S(2)}) async-start(), calls=%async_computation.8 | async-start | bytes 25165824 | tf_op jit(solution)/shard_map/reduce_scatter | solution.py:136
  370.7 866.6 %all-reduce.4.cloned.1.call-start = ((), (), s32[]{:S(2)}) async-start(), calls=%async_computation.9 | async-start | bytes 16777216 | tf_op jit(solution)/shard_map/psum | solution.py:144
  560.6 14.1 %all-to-all-start.3 = ((f32[16,256,2]{1,2,0:T(2,128)}), f32[16,256,2]{1,2,0:T(2,128)S(1)}, u32[]{:S(2)}, u32[]{:S(2)}) async-start(f32[16,256,2]{1,2,0:T(2,128)} %bitcast.20), calls=%async_computation.3 | async-start | bytes 65536 | tf_op jit(solution)/shard_map/all_to_all | solution.py:127
  574.7 36.0 %all-to-all-start.4 = ((bf16[16,256,256]{2,1,0:T(8,128)(2,1)}), bf16[16,256,256]{2,1,0:T(8,128)(2,1)S(1)}, u32[]{:S(2)}, u32[]{:S(2)}) async-start(bf16[16,256,256]{2,1,0:T(8,128)(2,1)} %copy.98), calls=%async_computation.4 | async-start | bytes 4194304 | tf_op jit(solution)/shard_map/all_to_all | solution.py:117
Sparse Core Ops, SparseCore 0:
  9.7 123.2 all-gather.1
  370.8 189.6 reduce-scatter.1
  563.2 674.0 all-reduce.3
where the time goes:
time: 1260 us
  waiting for transfers between devices  985 us (78%)
  matrix products  81.7 us (6%)
  blocking collectives  58.8 us (5%)
  local copies, waits for them, and re-layouts  51.6 us (4%)
  starting transfers between devices  34.4 us (3%)
  other arithmetic  31.4 us (2%)
  between operations  13.9 us (1%)
    psum x1, waiting for transfers between devices, shards(): summed = lax.psum(term_rows, ('seq', 'dp'))  620 us
    reduce_scatter x1, waiting for transfers between devices, shards(): lax.psum_scatter(lax.dot_general(columns, key_grad_low, (((0,), (0,)), ((...  190 us
    all_gather x1, waiting for transfers between devices, shards(): lax.all_gather(key_weight, 'fsdp', axis=0, tiled=True)  115 us
    all_to_all x1, blocking collectives, shards(): lax.all_to_all(grad_key.reshape(seq_len, key_count * HD), 'seq', split_ax...  58.8 us
    all_to_all x1, waiting for transfers between devices, shards(): lax.all_to_all(grad_query.reshape(seq_len, share * HD), 'seq', split_axis...  29.5 us
    dot_general x8, matrix products, one_block(): jnp.einsum('kgrw,rkgd->wkd', slope, query_block, preferred_element_type=j...  29.3 us
    all_to_all x1, waiting for transfers between devices, shards(): lax.all_to_all(outgoing, 'seq', split_axis=1, concat_axis=0, tiled=True)  28.5 us
  transfers between devices with their start and end apart: 8, of which 6 were waited for; matrix products, arithmetic and copies ran while one was open for 3% of the time, Pallas kernels for 0%

commit v1 on v0

--- a/solution.py
+++ b/solution.py
@@ -141,7 +141,7 @@
         scatter_dimension=0,
         tiled=True,
     )
-    summed = lax.psum(term_rows, ("seq", "dp"))
+    summed = lax.psum(lax.psum(term_rows, "seq"), "dp")
     norm_factor = (seq_len * lax.axis_size("fsdp") * lax.axis_size("dp")) ** (-0.5)
     weight_grad = (summed * norm_factor).astype(jnp.bfloat16)
     return (

time: 1260 us -> 913 us (0.72)
  waiting for transfers between devices: 985 us -> 639 us
    psum x1 -> x2, waiting for transfers between devices: 620 us -> 276 us  [shards(): summed = lax.psum(lax.psum(term_rows, 'seq'), 'dp')]
  transfers between devices with their start and end apart: 8 -> 9, of which waited for: 6 -> 7; matrix products, arithmetic and copies ran while one was open for 3% -> 4% of each run, Pallas kernels for 0% -> 0%
where the time goes in v1:
time: 913 us; the launch traced here: 911 us
  waiting for transfers between devices  639 us (70%)
  matrix products  81.7 us (9%)
  blocking collectives  58.8 us (6%)
  local copies, waits for them, and re-layouts  51.7 us (6%)
  starting transfers between devices  33.9 us (4%)
  other arithmetic  31.3 us (3%)
  between operations  13.9 us (2%)
    psum x2, waiting for transfers between devices, shards(): summed = lax.psum(lax.psum(term_rows, 'seq'), 'dp')  276 us
    reduce_scatter x1, waiting for transfers between devices, shards(): lax.psum_scatter(lax.dot_general(columns, key_grad_low, (((0,), (0,)), ((...  190 us
    all_gather x1, waiting for transfers between devices, shards(): lax.all_gather(key_weight, 'fsdp', axis=0, tiled=True)  115 us
    all_to_all x1, blocking collectives, shards(): lax.all_to_all(grad_key.reshape(seq_len, key_count * HD), 'seq', split_ax...  58.8 us
    dot_general x8, matrix products, one_block(): jnp.einsum('kgrw,rkgd->wkd', slope, query_block, preferred_element_type=j...  29.3 us
    all_to_all x1, waiting for transfers between devices, shards(): lax.all_to_all(grad_query.reshape(seq_len, share * HD), 'seq', split_axis...  28.7 us
    all_to_all x1, waiting for transfers between devices, shards(): lax.all_to_all(outgoing, 'seq', split_axis=1, concat_axis=0, tiled=True)  28.5 us
    dot_general x8, matrix products, one_block(): jnp.einsum('kgrw,wkd->rkgd', slope, key_block, preferred_element_type=jnp...  19.7 us
  transfers between devices with their start and end apart: 9, of which 7 were waited for; matrix products, arithmetic and copies ran while one was open for 4% of the time, Pallas kernels for 0%

profile of v1, /device:TPU:0, one launch (start us, length us, event | category | flops | bytes accessed | tf_op | source)
XLA Modules:
  0.0 910.6 jit_solution(6381320456182857525)
XLA Ops:
  8.8 2.4 copy.83
  11.2 7.1 all-to-all-start.1
  18.3 114.7 %all-gather.2.cloned.1.call-done = bf16[8192,512]{1,0:T(8,128)(2,1)} async-done(((bf16[4096,512]{1,0:T(8,128)(2,1)}), bf16[8192,512]{1,0:T(8,128)(2,1)}) %all-gather.2.cloned.1.call-update) | async-done | bytes 8388624 | tf_op jit(solution)/shard_map/all_gather | solution.py:93
  133.0 7.0 fusion.41
  140.1 1.6 broadcast_in_dim.83
  141.7 8.3 all-to-all-start
  150.9 28.5 %all-to-all-done = bf16[256,16,256]{0,2,1:T(8,128)(2,1)} async-done(((bf16[256,16,256]{0,2,1:T(8,128)(2,1)}), bf16[256,16,256]{0,2,1:T(8,128)(2,1)}, u32[]{:S(2)}, u32[]{:S(2)}) %all-to-all-start) | async-done | bytes 2097184 | tf_op jit(solution)/shard_map/all_to_all | solution.py:105
  179.3 6.3 all-to-all-start.2
  186.0 2.5 copy.84
  188.5 4.2 reshape.222
  192.7 4.1 copy.82
  196.8 2.9 reshape.221
  199.7 1.5 concatenate.7
  202.1 2.3 broadcast_in_dim.81
  204.4 88.0 %while.19 = (s32[]{:T(128)}, f32[4096,2,1]{0,1,2:T(2,128)}, bf16[4096,2,1,128]{0,3,1,2:T(8,128)(2,1)S(1)}, f32[4352,2,128]{0,2,1:T(8,128)}, s32[4096]{0:T(1024)S...) while((s32[]{:T(128)}, f32[4096,2,1]{0,1,2:T(2,128)}, ...), condition=%wide.region_6.7_spmd, body=%wide.region_2.6_spmd.sunk | while | flops 630850816 | bytes 21601552 | solution.py:79
  205.0 1.9 fusion.58
  207.6 1.0 select_reduce_fusion.2
  209.3 2.5 fusion.60
  211.7 3.7 fusion.61
  216.0 1.9 fusion.58
  218.6 1.0 select_reduce_fusion.2
  220.3 2.5 fusion.60
  222.7 3.6 fusion.61
  226.9 1.9 fusion.58
  229.6 1.0 select_reduce_fusion.2
  231.2 2.5 fusion.60
  233.7 3.7 fusion.61
  237.9 1.9 fusion.58
  242.3 2.5 fusion.60
  244.7 3.7 fusion.61
  248.9 1.9 fusion.58
  253.3 2.5 fusion.60
  255.7 3.7 fusion.61
  259.9 1.9 fusion.58
  262.6 1.0 select_reduce_fusion.2
  264.3 2.5 fusion.60
  266.7 3.7 fusion.61
  270.9 1.9 fusion.58
  273.6 1.0 select_reduce_fusion.2
  275.3 2.5 fusion.60
  277.7 3.7 fusion.61
  281.9 1.9 fusion.58
  284.6 1.0 select_reduce_fusion.2
  286.3 2.5 fusion.60
  288.7 3.7 fusion.61
  292.4 2.5 slice.3
  294.9 1.7 copy.102
  296.6 2.4 copy.90
  299.1 58.8 %all_to_all.93 = f32[16,256,256]{1,2,0:T(8,128)} all-to-all(f32[16,256,256]{1,2,0:T(8,128)S(1)} %copy.90), channel_id=1, replica_groups=mesh['seq'=16,'fsdp'=2,'dp'=4] {'seq'}, dimensions={0} | all-to-all | bytes 8388608 | tf_op jit(solution)/shard_map/all_to_all | solution.py:120
  357.9 2.5 reduce_sum.41
  360.4 10.3 %convolution_bitcast_fusion = f32[8192,512]{0,1:T(8,128)} fusion(bf16[256,512]{0,1:T(8,128)(2,1)S(1)} %bitcast.150, bf16[1,256,8192]{2,1,0:T(8,128)(2,1)} %param.8), kind=kOutput, calls=%fused_computation.33 | convolution fusion | flops 2147483648 | bytes 21233664 | tf_op jit(solution)/shard_map/dot_general | solution.py:137
  370.7 189.8 %reduce-scatter.2.cloned.1.call-done = f32[4096,512]{0,1:T(8,128)} async-done(((f32[8192,512]{0,1:T(8,128)}), f32[4096,512]{0,1:T(8,128)}) %reduce-scatter.2.cloned.1.call-update) | async-done | bytes 8388624 | tf_op jit(solution)/shard_map/reduce_scatter | solution.py:136
  560.6 167.4 %all-reduce.5.cloned.1.call-done = f32[4096,512]{0,1:T(8,128)} async-done(((f32[4096,512]{0,1:T(8,128)}), f32[4096,512]{0,1:T(8,128)}) %all-reduce.5.cloned.1.call-update) | async-done | bytes 8388624 | tf_op jit(solution)/shard_map/psum | solution.py:144
  728.1 5.8 all-to-all-start.3
  733.9 2.0 copy.101
  735.9 4.3 copy.98
  740.2 1.3 all-to-all-done.3
  741.5 6.0 all-to-all-start.4
  748.2 28.7 %all-to-all-done.4 = bf16[16,256,256]{2,1,0:T(8,128)(2,1)S(1)} async-done(((bf16[16,256,256]{2,1,0:T(8,128)(2,1)}), bf16[16,256,256]{2,1,0:T(8,128)(2,1)S(1)}, u32[]{:S(2)}, u32[]{:S(2)}) %all-to-all-start.4) | async-done | bytes 2097184 | tf_op jit(solution)/shard_map/all_to_all | solution.py:117
  776.8 2.4 copy.89
  779.2 4.1 copy.91
  783.3 108.1 %all-reduce.7.cloned.1.call-done = f32[4096,512]{0,1:T(8,128)} async-done(((f32[4096,512]{0,1:T(8,128)}), f32[4096,512]{0,1:T(8,128)}) %all-reduce.7.cloned.1.call-update) | async-done | bytes 8388624 | tf_op jit(solution)/shard_map/psum | solution.py:144
  891.3 6.3 multiply_convert_fusion
  897.7 6.4 copy.92
  (92 shorter events, 21.8 us)
Async XLA Ops:
  7.2 1.6 copy-start
  7.2 125.8 %all-gather.2.cloned.1.call-start = ((), (), s32[]{:S(2)}) async-start(), calls=%async_computation.7 | async-start | bytes 12582912 | tf_op jit(solution)/shard_map/all_gather | solution.py:93
  11.2 128.9 %all-to-all-start.1 = ((bf16[256,16,256]{0,2,1:T(8,128)(2,1)}), bf16[256,16,256]{0,2,1:T(8,128)(2,1)S(1)}, u32[]{:S(2)}, u32[]{:S(2)}) async-start(bf16[256,16,256]{0,2,1:T(8,128)(2,1)} %bitcast.144), calls=%async_computation.1 | async-start | bytes 4194304 | tf_op jit(solution)/shard_map/all_to_all | solution.py:104
  140.1 9.9 %copy-start.2 = (s32[1,32]{1,0:T(1,128)S(1)}, s32[1,32]{1,0:T(1,128)}, u32[]{:S(2)}) copy-start(s32[1,32]{1,0:T(1,128)} %param.10) | copy-start | bytes 388
  140.1 10.1 %copy-start.1 = (bf16[1,256,32]{1,2,0:T(8,128)(2,1)S(1)}, bf16[1,256,32]{1,2,0:T(8,128)(2,1)}, u32[]{:S(2)}) copy-start(bf16[1,256,32]{1,2,0:T(8,128)(2,1)} %param.11) | copy-start | bytes 49156
  141.7 37.6 %all-to-all-start = ((bf16[256,16,256]{0,2,1:T(8,128)(2,1)}), bf16[256,16,256]{0,2,1:T(8,128)(2,1)}, u32[]{:S(2)}, u32[]{:S(2)}) async-start(bf16[256,16,256]{0,2,1:T(8,128)(2,1)} %bitcast.145), calls=%async_computation | async-start | bytes 4194304 | tf_op jit(solution)/shard_map/all_to_all | solution.py:105
  179.3 21.9 %all-to-all-start.2 = ((bf16[256,16,2]{0,2,1:T(2,128)(2,1)}), bf16[256,16,2]{0,2,1:T(2,128)(2,1)S(1)}, u32[]{:S(2)}, u32[]{:S(2)}) async-start(bf16[256,16,2]{0,2,1:T(2,128)(2,1)} %all_to_all.76), calls=%async_computation.2 | async-start | bytes 32768 | tf_op jit(solution)/shard_map/all_to_all | solution.py:106
  185.6 374.9 %reduce-scatter.2.cloned.1.call-start = ((), (), s32[]{:S(2)}) async-start(), calls=%async_computation.8 | async-start | bytes 25165824 | tf_op jit(solution)/shard_map/reduce_scatter | solution.py:136
  370.7 357.4 %all-reduce.5.cloned.1.call-start = ((), (), s32[]{:S(2)}) async-start(), calls=%async_computation.9 | async-start | bytes 16777216 | tf_op jit(solution)/shard_map/psum | solution.py:144
  560.6 330.8 %all-reduce.7.cloned.1.call-start = ((), (), s32[]{:S(2)}) async-start(), calls=%async_computation.10 | async-start | bytes 16777216 | tf_op jit(solution)/shard_map/psum | solution.py:144
  728.1 13.4 %all-to-all-start.3 = ((f32[16,256,2]{1,2,0:T(2,128)}), f32[16,256,2]{1,2,0:T(2,128)S(1)}, u32[]{:S(2)}, u32[]{:S(2)}) async-start(f32[16,256,2]{1,2,0:T(2,128)} %bitcast.20), calls=%async_computation.3 | async-start | bytes 65536 | tf_op jit(solution)/shard_map/all_to_all | solution.py:127
  741.5 35.3 %all-to-all-start.4 = ((bf16[16,256,256]{2,1,0:T(8,128)(2,1)}), bf16[16,256,256]{2,1,0:T(8,128)(2,1)S(1)}, u32[]{:S(2)}, u32[]{:S(2)}) async-start(bf16[16,256,256]{2,1,0:T(8,128)(2,1)} %copy.98), calls=%async_computation.4 | async-start | bytes 4194304 | tf_op jit(solution)/shard_map/all_to_all | solution.py:117
Sparse Core Ops, SparseCore 0:
  9.7 123.2 all-gather.1
  370.8 189.6 reduce-scatter.1
  563.2 164.7 all-reduce.4
  730.5 160.7 all-reduce.6
